TPU v7x, 32 devices: a whole 2x2x4 slice. The times are simulated.
32 devices in a mesh: groups: 2 (over x), dp: 16 (over z, y, core).
Axes of the slice: x: 2, y: 2, z: 4, core: 2. Of those that a mesh axis runs over, the one named last changes fastest.
Arguments:
- tokens: bfloat16 [24576, 1024], P(('groups', 'dp')), parts along dimension 0, may hold values from -6 to 6
- token_mask: int32 [32, 768], P(('groups', 'dp')), parts along dimension 0, may hold values 0 or 1
- span_ids: int32 [32, 768], P(('groups', 'dp')), parts along dimension 0, may hold values from 0 to 191, never falling along the last dimension, each value on 1 to 8 neighbouring positions
- norm_gain: float32 [1024], replicated, may hold values from 0.1 to 1.9
- norm_shift: float32 [1024], replicated, may hold values from -3 to 3
- w_up: bfloat16 [1024, 4096], P(None, 'dp'), may hold values from -0.1875 to 0.1875
- b_up: float32 [4096], replicated, may hold values from -3 to 3
- w_down: bfloat16 [4096, 1024], P(None, 'dp'), may hold values from -0.09375 to 0.09375
Outputs:
- whitened: float32 [6144, 1024], P(('groups', 'dp')), parts along dimension 0
There are 2 independent parts, one for each index of `groups`. A program takes and returns all parts, laid end to end along the dimension named above; an argument that names none is the same for every part. Nothing has to cross between parts.
Inputs may be any that keep to these rules, and one draw needn't show every extreme that they name: `span_ids`: in each row the span numbers never fall, every span 0 to 191 holds 1 to 8 tokens, and one holds exactly 8.
All inputs are finite; a program needn't handle non-finite values. No bound on the sum of `token_mask` on one device may be relied on, other than what follows from the above.
Results may differ from a plain program's by a relative error of at most 0.0095.
Values may be sent and summed in bfloat16 or wider, within the bound.
A program may use at most 128 MiB of HBM per device.

v0:
```python
import math

import jax
import jax.numpy as jnp
from jax import lax
from jax.sharding import PartitionSpec as P

SEG_DEV = 192


def on_device(tokens, token_mask, span_ids, norm_gain, norm_shift, w_up, b_up, w_down):
    values = tokens.astype(jnp.float32)
    center = jnp.mean(values, axis=1, keepdims=True)
    spread = jnp.mean((values - center) ** 2, axis=1, keepdims=True)
    normed = ((values - center) * lax.rsqrt(spread + 1e-05) * norm_gain + norm_shift).astype(
        jnp.bfloat16
    )
    up_full, down_full = (
        lax.all_gather(w_up, "dp", axis=1, tiled=True),
        lax.all_gather(w_down, "dp", axis=1, tiled=True),
    )
    before = jnp.dot(normed, up_full, preferred_element_type=jnp.float32) + b_up
    hidden = jax.nn.gelu(before, approximate=False).astype(jnp.bfloat16)
    projected = jnp.dot(hidden, down_full, preferred_element_type=jnp.float32)
    block_out = (values + projected).astype(jnp.bfloat16)
    labels = jnp.arange(SEG_DEV, dtype=jnp.int32)[:, None]
    select = (span_ids[0][None, :] == labels) & (token_mask[0][None, :] == 1)
    sums = jnp.dot(select.astype(jnp.bfloat16), block_out, preferred_element_type=jnp.float32)
    counts = jnp.sum(select.astype(jnp.float32), axis=1)
    pooled = (sums / jnp.maximum(counts, 1.0)[:, None]).astype(jnp.bfloat16)
    partial_gram = jnp.dot(pooled.T, pooled, preferred_element_type=jnp.float32)
    gram = lax.psum(partial_gram, "dp")
    lower = jnp.linalg.cholesky(gram)
    solved = jax.scipy.linalg.solve_triangular(lower, pooled.astype(jnp.float32).T, lower=True)
    total_rows = SEG_DEV * lax.axis_size("dp")
    return math.sqrt(total_rows) * solved.T


def solution(mesh):
    in_specs = (
        P(("groups", "dp"), None),
        P(("groups", "dp"), None),
        P(("groups", "dp"), None),
        P(),
        P(),
        P(None, "dp"),
        P(),
        P(None, "dp"),
    )
    out_specs = P(("groups", "dp"), None)
    return jax.shard_map(
        on_device, mesh=mesh, in_specs=in_specs, out_specs=out_specs, check_vma=False
    )
```

profile of v0, /device:TPU:0, one launch (start us, length us, event | category | flops | bytes accessed | tf_op | source)
XLA Modules:
  0.0 630.9 jit_solution(12674228877443732165)
XLA Ops:
  13.3 77.0 %all-gather.3.cloned.1.call-done = bf16[1024,4096]{1,0:T(8,128)(2,1)} async-done(((bf16[1024,256]{1,0:T(8,128)(2,1)}), bf16[1024,4096]{1,0:T(8,128)(2,1)}) %all-gather.3.cloned.1.call-update) | async-done | bytes 8388624 | tf_op jit(solution)/shard_map/all_gather | solution.py:19
  90.4 37.2 %fusion.2.clone.6 = bf16[768,4096]{1,0:T(8,128)(2,1)} fusion(bf16[1024,4096]{1,0:T(8,128)(2,1)} %all-gather.3.cloned.1.call-done, f32[4096]{0:T(1024)S(1)} %copy-done.2, bf16[768,1024]{1,0:T(8,128)(2,1)S(1)} %copy-done.1, f32[1024]{0:T(1024)S(1)} %copy-done.3, f32[1024]{0:T(1024)S(1)} %copy-done.4, ...), kind=kOutput, calls=%fused_computation.5.clone.clone.clone.clone.clone.1 | convolution fusion | flops 6654787584 | bytes 16283648 | tf_op jit(solution)/shard_map/dot_general | solution.py:22
  127.5 38.1 %all-gather.5.cloned.1.call-done = bf16[4096,1024]{0,1:T(8,128)(2,1)} async-done(((bf16[4096,64]{0,1:T(8,128)(2,1)}), bf16[4096,1024]{0,1:T(8,128)(2,1)}) %all-gather.5.cloned.1.call-update) | async-done | bytes 8388624 | tf_op jit(solution)/shard_map/all_gather | solution.py:20
  165.6 11.4 %fusion.49 = bf16[768,1024]{1,0:T(8,128)(2,1)S(1)} fusion(bf16[768,1024]{1,0:T(8,128)(2,1)S(1)} %copy-done.1, bf16[4096,1024]{0,1:T(8,128)(2,1)} %all-gather.5.cloned.1.call-done, bf16[768,4096]{1,0:T(8,128)(2,1)} %fusion.2.clone.6), kind=kOutput, calls=%fused_computation.66 | convolution fusion | flops 6444810240 | bytes 17825792 | tf_op jit(solution)/shard_map/dot_general | solution.py:24
  180.3 109.8 %all-reduce.3.cloned.1.call-done = f32[1024,1024]{0,1:T(8,128)} async-done(((f32[1024,1024]{0,1:T(8,128)}), f32[1024,1024]{0,1:T(8,128)}) %all-reduce.3.cloned.1.call-update) | async-done | bytes 4194320 | tf_op jit(solution)/shard_map/psum | solution.py:32
  290.2 5.3 copy.12
  301.9 11.7 %cholesky.223 = f32[128,128]{1,0:T(8,128)S(1)} custom-call(f32[128,128]{1,0:T(8,128)S(1)} %cholesky.580), custom_call_target="Cholesky" | custom-call | tf_op jit(solution)/shard_map/jit(cholesky)/cholesky | solution.py:33
  313.6 9.8 %custom-call.63 = f32[1,128,128]{1,2,0:T(8,128)S(1)} custom-call(f32[1,128,128]{2,1,0:T(8,128)S(1)} %get-tuple-element.69), custom_call_target="InvertDiagBlocksLowerTriangular" | custom-call | tf_op jit(solution)/shard_map/jit(cholesky)/cholesky | solution.py:33
  329.9 11.9 %cholesky.244 = f32[128,128]{1,0:T(8,128)S(1)} custom-call(f32[128,128]{1,0:T(8,128)S(1)} %cholesky.584), custom_call_target="Cholesky" | custom-call | tf_op jit(solution)/shard_map/jit(cholesky)/cholesky | solution.py:33
  342.4 9.8 %custom-call.64 = f32[1,128,128]{1,2,0:T(8,128)S(1)} custom-call(f32[1,128,128]{2,1,0:T(8,128)S(1)} %get-tuple-element.66), custom_call_target="InvertDiagBlocksLowerTriangular" | custom-call | tf_op jit(solution)/shard_map/jit(cholesky)/cholesky | solution.py:33
  355.6 11.7 %cholesky.468 = f32[128,128]{1,0:T(8,128)S(1)} custom-call(f32[128,128]{1,0:T(8,128)S(1)} %cholesky.589), custom_call_target="Cholesky" | custom-call | tf_op jit(solution)/shard_map/jit(cholesky)/cholesky | solution.py:33
  368.5 9.8 %custom-call.65 = f32[1,128,128]{1,2,0:T(8,128)S(1)} custom-call(f32[1,128,128]{2,1,0:T(8,128)S(1)} %get-tuple-element.63), custom_call_target="InvertDiagBlocksLowerTriangular" | custom-call | tf_op jit(solution)/shard_map/jit(cholesky)/cholesky | solution.py:33
  381.8 11.9 %cholesky.487 = f32[128,128]{1,0:T(8,128)S(1)} custom-call(f32[128,128]{1,0:T(8,128)S(1)} %cholesky.594), custom_call_target="Cholesky" | custom-call | tf_op jit(solution)/shard_map/jit(cholesky)/cholesky | solution.py:33
  395.0 9.8 %custom-call.66 = f32[1,128,128]{1,2,0:T(8,128)S(1)} custom-call(f32[1,128,128]{2,1,0:T(8,128)S(1)} %get-tuple-element.60), custom_call_target="InvertDiagBlocksLowerTriangular" | custom-call | tf_op jit(solution)/shard_map/jit(cholesky)/cholesky | solution.py:33
  408.3 11.7 %cholesky.506 = f32[128,128]{1,0:T(8,128)S(1)} custom-call(f32[128,128]{1,0:T(8,128)S(1)} %cholesky.599), custom_call_target="Cholesky" | custom-call | tf_op jit(solution)/shard_map/jit(cholesky)/cholesky | solution.py:33
  421.3 10.2 %custom-call.67 = f32[1,128,128]{1,2,0:T(8,128)S(1)} custom-call(f32[1,128,128]{2,1,0:T(8,128)S(1)} %get-tuple-element.57), custom_call_target="InvertDiagBlocksLowerTriangular" | custom-call | tf_op jit(solution)/shard_map/jit(cholesky)/cholesky | solution.py:33
  434.8 11.7 %cholesky.526 = f32[128,128]{1,0:T(8,128)S(1)} custom-call(f32[128,128]{1,0:T(8,128)S(1)} %cholesky.604), custom_call_target="Cholesky" | custom-call | tf_op jit(solution)/shard_map/jit(cholesky)/cholesky | solution.py:33
  447.8 9.8 %custom-call.68 = f32[1,128,128]{1,2,0:T(8,128)S(1)} custom-call(f32[1,128,128]{2,1,0:T(8,128)S(1)} %get-tuple-element.54), custom_call_target="InvertDiagBlocksLowerTriangular" | custom-call | tf_op jit(solution)/shard_map/jit(cholesky)/cholesky | solution.py:33
  460.6 11.9 %cholesky.546 = f32[128,128]{1,0:T(8,128)S(1)} custom-call(f32[128,128]{1,0:T(8,128)S(1)} %cholesky.609), custom_call_target="Cholesky" | custom-call | tf_op jit(solution)/shard_map/jit(cholesky)/cholesky | solution.py:33
  473.7 9.8 %custom-call.69 = f32[1,128,128]{1,2,0:T(8,128)S(1)} custom-call(f32[1,128,128]{2,1,0:T(8,128)S(1)} %get-tuple-element.51), custom_call_target="InvertDiagBlocksLowerTriangular" | custom-call | tf_op jit(solution)/shard_map/jit(cholesky)/cholesky | solution.py:33
  486.1 11.7 %cholesky.564 = f32[128,128]{1,0:T(8,128)S(1)} custom-call(f32[128,128]{1,0:T(8,128)S(1)} %convolution_subtract_fusion.13), custom_call_target="Cholesky" | custom-call | tf_op jit(solution)/shard_map/jit(cholesky)/cholesky | solution.py:33
  504.7 4.8 select_select_fusion
  509.5 22.8 %while.1 = (s32[]{:T(128)}, f32[1024,1024]{1,0:T(8,128)}, s32[8,2]{0,1:T(2,128)S(1)}, f32[8,128,128]{2,1,0:T(8,128)S(1)}, s32[]{:T(128)}) while((s32[]{:T(128)}, f32[1024,1024]{1,0:T(8,128)}, s32[8,2]{0,1:T(2,128)S(1)}, f32[8,128,128]{2,1,0:T(8,128)S(1)}, s32[]{:T(128)}) %tuple.58), condition=%wide.while_cond, body=%wide.while_body.sunk | while | flops 2 | bytes 131181 | solution.py:34
  532.3 78.8 %custom-call.70 = f32[8,128,128]{1,2,0:T(8,128)S(1)} custom-call(f32[8,128,128]{2,1,0:T(8,128)S(1)} %get-tuple-element.12), custom_call_target="InvertDiagBlocksLowerTriangular" | custom-call | tf_op jit(solution)/shard_map/jit(_solve_triangular)/triangular_solve | solution.py:34
  (107 shorter events, 86.6 us)
Async XLA Ops:
  6.5 83.8 %copy-start.1 = (bf16[768,1024]{1,0:T(8,128)(2,1)S(1)}, bf16[768,1024]{1,0:T(8,128)(2,1)}, u32[]{:S(2)}) copy-start(bf16[768,1024]{1,0:T(8,128)(2,1)} %param.8) | copy-start | bytes 4718596
  6.5 83.8 %copy-start.4 = (f32[1024]{0:T(1024)S(1)}, f32[1024]{0:T(1024)}, u32[]{:S(2)}) copy-start(f32[1024]{0:T(1024)} %param.11) | copy-start | bytes 12292
  6.5 83.8 %copy-start.3 = (f32[1024]{0:T(1024)S(1)}, f32[1024]{0:T(1024)}, u32[]{:S(2)}) copy-start(f32[1024]{0:T(1024)} %param.12) | copy-start | bytes 12292
  6.5 83.8 %copy-start.2 = (f32[4096]{0:T(1024)S(1)}, f32[4096]{0:T(1024)}, u32[]{:S(2)}) copy-start(f32[4096]{0:T(1024)} %param.14) | copy-start | bytes 49156
  6.5 83.8 %all-gather.3.cloned.1.call-start = ((), (), s32[]{:S(2)}) async-start(), calls=%async_computation | async-start | bytes 8912896 | tf_op jit(solution)/shard_map/all_gather | solution.py:19
  7.3 158.3 %all-gather.5.cloned.1.call-start = ((), (), s32[]{:S(2)}) async-start(), calls=%async_computation.1 | async-start | bytes 8912896 | tf_op jit(solution)/shard_map/all_gather | solution.py:20
  8.0 282.1 %all-reduce.3.cloned.1.call-start = ((), (), s32[]{:S(2)}) async-start(), calls=%async_computation.2 | async-start | bytes 8388608 | tf_op jit(solution)/shard_map/psum | solution.py:32
  299.9 1.9 copy-start
Sparse Core Ops, SparseCore 0:
  9.5 80.7 all-gather.2
  92.5 73.0 all-gather.4
  180.4 109.6 all-reduce.2
where the time goes:
time: 641 us; the launch traced here: 631 us
  other arithmetic  266 us (41%)
  waiting for transfers between devices  226 us (35%)
  matrix products  86.9 us (14%)
  local copies, waits for them, and re-layouts  32.5 us (5%)
  between operations  18.5 us (3%)
    another operation x30, other arithmetic, on_device(): lower = jnp.linalg.cholesky(gram)  172 us
    psum x1, waiting for transfers between devices, on_device(): gram = lax.psum(partial_gram, 'dp')  110 us
    another operation x3, other arithmetic, on_device(): jax.scipy.linalg.solve_triangular(lower, pooled.astype(jnp.float32).T, lo...  83.6 us
    all_gather x1, waiting for transfers between devices, on_device(): lax.all_gather(w_up, 'dp', axis=1, tiled=True)  77 us
    all_gather x1, waiting for transfers between devices, on_device(): lax.all_gather(w_down, 'dp', axis=1, tiled=True)  38.1 us
    dot_general x1, matrix products, on_device(): before = jnp.dot(normed, up_full, preferred_element_type=jnp.float32) + b_up  37.2 us
    another operation x14, matrix products, on_device(): lower = jnp.linalg.cholesky(gram)  23.1 us
    another operation x24, local copies, waits for them, and re-layouts  22.7 us
  transfers between devices with their start and end apart: 3, of which 3 were waited for; matrix products, arithmetic and copies ran while one was open for 7% of the time, Pallas kernels for 0%

commit v1 on v0

--- a/solution.py
+++ b/solution.py
@@ -1,11 +1,101 @@
+import functools
 import math
 
 import jax
 import jax.numpy as jnp
 from jax import lax
+from jax.experimental import pallas as pl
+from jax.experimental.pallas import tpu as pltpu
 from jax.sharding import PartitionSpec as P
 
 SEG_DEV = 192
+BLOCK = 128
+HIGHEST = lax.Precision.HIGHEST
+
+
+def inverse_factor(src, dst):
+    lane = lax.broadcasted_iota(jnp.int32, (8, BLOCK), 1)
+    sub = lax.broadcasted_iota(jnp.int32, (8, BLOCK), 0)
+    groups = BLOCK // 8
+    held = [src[8 * q : 8 * q + 8, :BLOCK] for q in range(groups)]
+
+    def column(block, c):
+        return jnp.broadcast_to(block[:, c : c + 1], (8, BLOCK))
+
+    def row(block, r):
+        return jnp.broadcast_to(block[r : r + 1, :], (8, BLOCK))
+
+    for p in range(groups):
+        at = 8 * p
+        inside = (lane >= at) & (lane < at + 8)
+        raw = held[p]
+        cols = [column(raw, at + c) for c in range(8)]
+        work = jnp.where(inside, jnp.where(lane - at == sub, 1.0, 0.0), raw)
+        done = jnp.zeros((8, BLOCK), jnp.float32)
+        for j in range(8):
+            here = sub == j
+            pivot = row(cols[j], j)
+            inv = 1.0 / pivot
+            done = jnp.where(here, work * lax.rsqrt(pivot), done)
+            scaled = row(work, j) * inv
+            work = jnp.where(here, scaled, work - cols[j] * scaled)
+            for c in range(j + 1, 8):
+                scaled = row(cols[c], j) * inv
+                cols[c] = jnp.where(here, scaled, cols[c] - cols[j] * scaled)
+        dst[at : at + 8, :] = jnp.where(lane <= at + sub, done, 0.0)
+        rows = [row(work, c) for c in range(8)]
+        for q in range(p + 1, groups):
+            total = jnp.where(inside, 0.0, held[q])
+            for c in range(8):
+                total = total - column(held[q], at + c) * rows[c]
+            held[q] = total
+
+
+def whiten_kernel(scale, gram_ref, rows_ref, out_ref, a, panel, inv):
+    n = gram_ref.shape[0]
+    extra = rows_ref.shape[1]
+    a[:, :n] = gram_ref[...]
+    a[:, n:] = jnp.zeros((n, a.shape[1] - n), jnp.float32)
+    a[:, n : n + extra] = rows_ref[...]
+    blocks = n // BLOCK
+
+    def step(k, carry):
+        lo = pl.multiple_of(k * BLOCK, BLOCK)
+        panel[:, :BLOCK] = a[pl.ds(lo, BLOCK), pl.ds(lo, BLOCK)]
+        inverse_factor(panel, inv)
+        panel[...] = jnp.dot(
+            inv[...], a[pl.ds(lo, BLOCK), :], preferred_element_type=jnp.float32, precision=HIGHEST
+        )
+        out_ref[pl.ds(lo, BLOCK), :] = panel[:, n : n + extra] * scale
+
+        def trail(i, carry):
+            hi = pl.multiple_of(i * BLOCK, BLOCK)
+            left = panel[:, pl.ds(hi, BLOCK)].T
+            a[pl.ds(hi, BLOCK), :] -= jnp.dot(
+                left, panel[...], preferred_element_type=jnp.float32, precision=HIGHEST
+            )
+            return carry
+
+        return lax.fori_loop(k + 1, blocks, trail, carry)
+
+    lax.fori_loop(0, blocks, step, 0)
+
+
+def whiten(gram, rows_t, scale):
+    n, extra = rows_t.shape
+    wide = n + (extra + BLOCK - 1) // BLOCK * BLOCK
+    return pl.pallas_call(
+        functools.partial(whiten_kernel, scale),
+        out_shape=jax.ShapeDtypeStruct((n, extra), jnp.float32),
+        in_specs=[pl.BlockSpec(memory_space=pltpu.VMEM)] * 2,
+        out_specs=pl.BlockSpec(memory_space=pltpu.VMEM),
+        scratch_shapes=[
+            pltpu.VMEM((n, wide), jnp.float32),
+            pltpu.VMEM((BLOCK, wide), jnp.float32),
+            pltpu.VMEM((BLOCK, BLOCK), jnp.float32),
+        ],
+        compiler_params=pltpu.CompilerParams(vmem_limit_bytes=32 << 20),
+    )(gram, rows_t)
 
 
 def on_device(tokens, token_mask, span_ids, norm_gain, norm_shift, w_up, b_up, w_down):
@@ -28,12 +118,12 @@
     sums = jnp.dot(select.astype(jnp.bfloat16), block_out, preferred_element_type=jnp.float32)
     counts = jnp.sum(select.astype(jnp.float32), axis=1)
     pooled = (sums / jnp.maximum(counts, 1.0)[:, None]).astype(jnp.bfloat16)
-    partial_gram = jnp.dot(pooled.T, pooled, preferred_element_type=jnp.float32)
-    gram = lax.psum(partial_gram, "dp")
-    lower = jnp.linalg.cholesky(gram)
-    solved = jax.scipy.linalg.solve_triangular(lower, pooled.astype(jnp.float32).T, lower=True)
+    every = lax.all_gather(pooled, "dp", axis=0, tiled=True)
+    gram = lax.dot_general(
+        every, every, (((0,), (0,)), ((), ())), preferred_element_type=jnp.float32
+    )
     total_rows = SEG_DEV * lax.axis_size("dp")
-    return math.sqrt(total_rows) * solved.T
+    return whiten(gram, pooled.astype(jnp.float32).T, math.sqrt(total_rows)).T
 
 
 def solution(mesh):

time: 641 us -> 321 us (0.50); the launches traced: 631 us -> 321 us
  other arithmetic: 266 us -> 5.32 us
  Pallas kernels: 0 us -> 63.4 us
  waiting for transfers between devices: 226 us -> 177 us
  local copies, waits for them, and re-layouts: 32.5 us -> 2.14 us
  matrix products: 86.9 us -> 59.9 us
    another operation x33 -> x0, other arithmetic: 256 us -> none  [the longest x30 172 us: on_device(): lower = jnp.linalg.cholesky(gram)]
    psum x1 -> x0, waiting for transfers between devices: 110 us -> none  [on_device(): gram = lax.psum(partial_gram, 'dp')]
    pallas_call x0 -> x1, Pallas kernels: none -> 63.4 us  [whiten(): pl.pallas_call(functools.partial(whiten_kernel, scale), out_shape=jax.Sha...]
    all_gather x0 -> x1, waiting for transfers between devices: none -> 60.2 us  [on_device(): every = lax.all_gather(pooled, 'dp', axis=0, tiled=True)]
    another operation x29 -> x0, matrix products: 35 us -> none  [the longest x14 23.1 us: on_device(): lower = jnp.linalg.cholesky(gram)]
    another operation x33 -> x0, local copies, waits for them, and re-layouts: 25.2 us -> none
    dot_general x1, matrix products: 2.73 us -> 10.7 us  [on_device(): lax.dot_general(every, every, (((0,), (0,)), ((), ())), preferred_element...]
  transfers between devices with their start and end apart: 3 -> 3, of which waited for: 3 -> 3; matrix products, arithmetic and copies ran while one was open for 7% -> 13% of each run, Pallas kernels for 0% -> 0%
where the time goes in v1:
time: 321 us
  waiting for transfers between devices  177 us (55%)
  Pallas kernels  63.4 us (20%)
  matrix products  59.9 us (19%)
  between operations  13.2 us (4%)
  other arithmetic  5.32 us (2%)
    all_gather x1, waiting for transfers between devices, on_device(): lax.all_gather(w_up, 'dp', axis=1, tiled=True)  77 us
    pallas_call x1, Pallas kernels, whiten(): pl.pallas_call(functools.partial(whiten_kernel, scale), out_shape=jax.Sha...  63.4 us
    all_gather x1, waiting for transfers between devices, on_device(): every = lax.all_gather(pooled, 'dp', axis=0, tiled=True)  60.2 us
    all_gather x1, waiting for transfers between devices, on_device(): lax.all_gather(w_down, 'dp', axis=1, tiled=True)  38 us
    dot_general x1, matrix products, on_device(): before = jnp.dot(normed, up_full, preferred_element_type=jnp.float32) + b_up  37.3 us
    dot_general x1, matrix products, on_device(): projected = jnp.dot(hidden, down_full, preferred_element_type=jnp.float32)  11.2 us
    dot_general x1, matrix products, on_device(): lax.dot_general(every, every, (((0,), (0,)), ((), ())), preferred_element...  10.7 us
  transfers between devices with their start and end apart: 3, of which 3 were waited for; matrix products, arithmetic and copies ran while one was open for 13% of the time, Pallas kernels for 0%

profile of v1, /device:TPU:0, one launch (start us, length us, event | category | flops | bytes accessed | tf_op | source)
XLA Modules:
  0.0 320.6 jit_solution(9702496194479670412)
XLA Ops:
  6.5 0.0 all-gather.4.cloned.1.call-start
  6.5 0.7 all-gather.4.cloned.1.call-update
  7.3 0.0 all-gather.6.cloned.1.call-start
  7.3 0.7 all-gather.6.cloned.1.call-update
  8.0 0.0 all-gather.8.cloned.1.call-start
  8.1 0.7 reduce
  8.8 0.7 compare_reduce_fusion
  9.5 0.2 convert_reduce_fusion.1
  9.6 1.7 convert_reduce_fusion
  11.3 2.0 fusion.44
  13.3 0.0 copy-start
  13.3 77.0 %all-gather.4.cloned.1.call-done = bf16[1024,4096]{1,0:T(8,128)(2,1)} async-done(((bf16[1024,256]{1,0:T(8,128)(2,1)}), bf16[1024,4096]{1,0:T(8,128)(2,1)}) %all-gather.4.cloned.1.call-update) | async-done | bytes 8388624 | tf_op jit(solution)/shard_map/all_gather | solution.py:109
  90.3 37.3 %fusion.2.clone.6 = bf16[768,4096]{1,0:T(8,128)(2,1)} fusion(bf16[1024,4096]{1,0:T(8,128)(2,1)} %all-gather.4.cloned.1.call-done, f32[4096]{0:T(1024)} %param.14, bf16[768,1024]{1,0:T(8,128)(2,1)} %param.8, f32[1024]{0:T(1024)} %param.12, f32[1024]{0:T(1024)} %param.11, f32[768]{0:T(1024)S(1)} %add_rsqrt_fusion, ...), kind=kOutput, calls=%fused_computation.3.clone.clone.clone.clone.clone.1 | convolution fusion | flops 6654787584 | bytes 16283648 | tf_op jit(solution)/shard_map/dot_general | solution.py:112
  127.6 38.0 %all-gather.6.cloned.1.call-done = bf16[4096,1024]{0,1:T(8,128)(2,1)} async-done(((bf16[4096,64]{0,1:T(8,128)(2,1)}), bf16[4096,1024]{0,1:T(8,128)(2,1)}) %all-gather.6.cloned.1.call-update) | async-done | bytes 8388624 | tf_op jit(solution)/shard_map/all_gather | solution.py:110
  165.6 0.0 copy-done
  165.6 11.2 %fusion.48 = bf16[768,1024]{1,0:T(8,128)(2,1)S(1)} fusion(bf16[768,1024]{1,0:T(8,128)(2,1)S(1)} %copy-done, bf16[4096,1024]{0,1:T(8,128)(2,1)} %all-gather.6.cloned.1.call-done, bf16[768,4096]{1,0:T(8,128)(2,1)} %fusion.2.clone.6), kind=kOutput, calls=%fused_computation.60 | convolution fusion | flops 6444810240 | bytes 17825792 | tf_op jit(solution)/shard_map/dot_general | solution.py:114
  176.8 0.8 fusion.59
  177.6 0.9 copy.19
  178.5 0.0 all-gather.8.cloned.1.call-update
  178.5 0.1 convert_bitcast_fusion.rows_ref
  178.6 60.2 %all-gather.8.cloned.1.call-done = bf16[3072,1024]{1,0:T(8,128)(2,1)} async-done(((bf16[192,1024]{1,0:T(8,128)(2,1)}), bf16[3072,1024]{1,0:T(8,128)(2,1)}) %all-gather.8.cloned.1.call-update) | async-done | bytes 6291472 | tf_op jit(solution)/shard_map/all_gather | solution.py:121
  238.8 10.7 %fusion.94.gram_ref = f32[1024,1024]{1,0:T(8,128)S(1)} fusion(bf16[3072,1024]{1,0:T(8,128)(2,1)} %all-gather.8.cloned.1.call-done), kind=kOutput, calls=%fused_computation.107 | convolution fusion | flops 6442450944 | bytes 10485760 | tf_op jit(solution)/shard_map/dot_general | solution.py:122
  249.5 63.4 %shard_map.82 = f32[1024,192]{1,0:T(8,128)S(1)} custom-call(f32[1024,1024]{1,0:T(8,128)S(1)} %fusion.94.gram_ref, f32[1024,192]{1,0:T(8,128)S(1)} %convert_bitcast_fusion.rows_ref), custom_call_target="tpu_custom_call" | custom-call | tf_op jit(solution)/shard_map/pallas_call | solution.py:87
  312.9 1.2 copy.20
  (3 shorter events, 0.0 us)
Async XLA Ops:
  6.5 83.8 %all-gather.4.cloned.1.call-start = ((), (), s32[]{:S(2)}) async-start(), calls=%async_computation | async-start | bytes 8912896 | tf_op jit(solution)/shard_map/all_gather | solution.py:109
  7.3 158.4 %all-gather.6.cloned.1.call-start = ((), (), s32[]{:S(2)}) async-start(), calls=%async_computation.1 | async-start | bytes 8912896 | tf_op jit(solution)/shard_map/all_gather | solution.py:110
  8.0 230.8 %all-gather.8.cloned.1.call-start = ((), (), s32[]{:S(2)}) async-start(), calls=%async_computation.2 | async-start | bytes 6684672 | tf_op jit(solution)/shard_map/all_gather | solution.py:121
  13.3 152.3 %copy-start = (bf16[768,1024]{1,0:T(8,128)(2,1)S(1)}, bf16[768,1024]{1,0:T(8,128)(2,1)}, u32[]{:S(2)}) copy-start(bf16[768,1024]{1,0:T(8,128)(2,1)} %param.8) | copy-start | bytes 4718596
Sparse Core Ops, SparseCore 0:
  9.5 80.7 all-gather.3
  92.5 73.0 all-gather.5
  178.6 60.1 all-gather.7

commit v2 on v1

--- a/solution.py
+++ b/solution.py
@@ -98,6 +98,104 @@
     )(gram, rows_t)
 
 
+def ring_kernel(chips, count, *refs):
+    ins, outs = refs[:count], refs[count : 2 * count]
+    ring_send, ring_recv, core_send, core_recv, own_sem = refs[2 * count :]
+    me = lax.axis_index("dp")
+    core, chip = lax.rem(me, 2), me // 2
+    half = chips // 2
+    odd = lax.rem(chip, 2)
+    place = (1 - odd) * (chip // 2) + odd * (chips - 1 - chip // 2)
+    turn = 1 - 2 * core
+    partner = me + turn
+
+    def device(q):
+        q = lax.rem(q + 2 * chips, chips)
+        back = q // half
+        return 2 * ((1 - back) * 2 * q + back * (2 * (chips - 1 - q) + 1)) + core
+
+    ahead, behind = device(place + turn), device(place - turn)
+    barrier = pltpu.get_barrier_semaphore()
+    for other in (ahead, behind, partner):
+        pl.semaphore_signal(
+            barrier, inc=1, device_id={"dp": other}, device_id_type=pl.DeviceIdType.MESH
+        )
+    pl.semaphore_wait(barrier, 3)
+
+    steps = (half, chips - 1 - half)
+    started, across = [], []
+
+    def send(a, source, slot, way, step):
+        copy = pltpu.make_async_remote_copy(
+            src_ref=source,
+            dst_ref=outs[a].at[slot],
+            send_sem=ring_send.at[a, way, step],
+            recv_sem=ring_recv.at[a, way, step],
+            device_id={"dp": (ahead, behind)[way]},
+            device_id_type=pl.DeviceIdType.MESH,
+        )
+        copy.start()
+        started.append(copy)
+        return copy
+
+    def share(a, source, slot, index):
+        copy = pltpu.make_async_remote_copy(
+            src_ref=source,
+            dst_ref=outs[a].at[slot],
+            send_sem=core_send.at[a, index],
+            recv_sem=core_recv.at[a, index],
+            device_id={"dp": partner},
+            device_id_type=pl.DeviceIdType.MESH,
+        )
+        copy.start()
+        across.append(copy)
+
+    flying, local = {}, []
+    for a in range(count):
+        for way in range(2):
+            flying[a, way] = send(a, ins[a], me, way, 0)
+        share(a, ins[a], me, 0)
+        local.append(pltpu.make_async_copy(ins[a], outs[a].at[me], own_sem.at[a]))
+        local[-1].start()
+    for step in range(half):
+        for a in range(count):
+            for way in range(2):
+                if step >= steps[way]:
+                    continue
+                flying[a, way].wait_recv()
+                slot = device(place - (1 + step) * turn * (1 - 2 * way))
+                block = outs[a].at[slot]
+                if step + 1 < steps[way]:
+                    flying[a, way] = send(a, block, slot, way, step + 1)
+                share(a, block, slot, 1 + way * half + step)
+    for copy in local:
+        copy.wait()
+    for copy in started:
+        copy.wait_send()
+    for copy in across:
+        copy.wait()
+
+
+def ring_gather(blocks, collective_id):
+    devices = lax.axis_size("dp")
+    chips, count = devices // 2, len(blocks)
+    dma = pltpu.SemaphoreType.DMA
+    return pl.pallas_call(
+        functools.partial(ring_kernel, chips, count),
+        out_shape=[jax.ShapeDtypeStruct((devices,) + b.shape, b.dtype) for b in blocks],
+        in_specs=[pl.BlockSpec(memory_space=pl.ANY)] * count,
+        out_specs=[pl.BlockSpec(memory_space=pl.ANY)] * count,
+        scratch_shapes=[
+            dma((count, 2, chips // 2)),
+            dma((count, 2, chips // 2)),
+            dma((count, chips)),
+            dma((count, chips)),
+            dma((count,)),
+        ],
+        compiler_params=pltpu.CompilerParams(collective_id=collective_id, has_side_effects=True),
+    )(*blocks)
+
+
 def on_device(tokens, token_mask, span_ids, norm_gain, norm_shift, w_up, b_up, w_down):
     values = tokens.astype(jnp.float32)
     center = jnp.mean(values, axis=1, keepdims=True)
@@ -105,20 +203,25 @@
     normed = ((values - center) * lax.rsqrt(spread + 1e-05) * norm_gain + norm_shift).astype(
         jnp.bfloat16
     )
-    up_full, down_full = (
-        lax.all_gather(w_up, "dp", axis=1, tiled=True),
-        lax.all_gather(w_down, "dp", axis=1, tiled=True),
-    )
-    before = jnp.dot(normed, up_full, preferred_element_type=jnp.float32) + b_up
+    up_full, down_full = ring_gather((w_up.T, w_down.T), 0)
+    width, hidden_size = tokens.shape[1], b_up.shape[0]
+    up_full, down_full = up_full.reshape(hidden_size, width), down_full.reshape(width, hidden_size)
+    over_last = (((1,), (1,)), ((), ()))
+    before = (
+        lax.dot_general(normed, up_full, over_last, preferred_element_type=jnp.float32) + b_up
+    )
     hidden = jax.nn.gelu(before, approximate=False).astype(jnp.bfloat16)
-    projected = jnp.dot(hidden, down_full, preferred_element_type=jnp.float32)
+    projected = lax.dot_general(
+        hidden, down_full, over_last, preferred_element_type=jnp.float32
+    )
     block_out = (values + projected).astype(jnp.bfloat16)
     labels = jnp.arange(SEG_DEV, dtype=jnp.int32)[:, None]
     select = (span_ids[0][None, :] == labels) & (token_mask[0][None, :] == 1)
     sums = jnp.dot(select.astype(jnp.bfloat16), block_out, preferred_element_type=jnp.float32)
     counts = jnp.sum(select.astype(jnp.float32), axis=1)
     pooled = (sums / jnp.maximum(counts, 1.0)[:, None]).astype(jnp.bfloat16)
-    every = lax.all_gather(pooled, "dp", axis=0, tiled=True)
+    (every,) = ring_gather((pooled,), 1)
+    every = every.reshape(-1, width)
     gram = lax.dot_general(
         every, every, (((0,), (0,)), ((), ())), preferred_element_type=jnp.float32
     )

time: 321 us -> 258 us (0.80)
  waiting for transfers between devices: 177 us -> 0 us
  Pallas kernels: 63.4 us -> 191 us
  between operations: 13.2 us -> 0.12 us
    all_gather x3 -> x0, waiting for transfers between devices: 175 us -> none  [the longest x1 77 us: on_device(): lax.all_gather(w_up, 'dp', axis=1, tiled=True)]
    pallas_call x0 -> x2, Pallas kernels: none -> 128 us  [ring_gather(): pl.pallas_call(functools.partial(ring_kernel, chips, count), out_shape=[j...]
  transfers between devices with their start and end apart: 3 -> 0, of which waited for: 3 -> 0; matrix products, arithmetic and copies ran while one was open for 13% -> 0% of each run, Pallas kernels for 0% -> 0%
where the time goes in v2:
time: 258 us
  Pallas kernels  191 us (74%)
  matrix products  58.2 us (23%)
  local copies, waits for them, and re-layouts  4.2 us (2%)
  other arithmetic  3.96 us (2%)
    pallas_call x2, Pallas kernels, ring_gather(): pl.pallas_call(functools.partial(ring_kernel, chips, count), out_shape=[j...  128 us
    pallas_call x1, Pallas kernels, whiten(): pl.pallas_call(functools.partial(whiten_kernel, scale), out_shape=jax.Sha...  63.4 us
    dot_general x1, matrix products, on_device(): lax.dot_general(normed, up_full, over_last, preferred_element_type=jnp.fl...  37.7 us
    dot_general x1, matrix products, on_device(): lax.dot_general(every, every, (((0,), (0,)), ((), ())), preferred_element...  10.7 us
    dot_general x1, matrix products, on_device(): lax.dot_general(hidden, down_full, over_last, preferred_element_type=jnp....  9.09 us

profile of v2, /device:TPU:0, one launch (start us, length us, event | category | flops | bytes accessed | tf_op | source)
XLA Modules:
  0.0 258.0 jit_solution(9718411198344069558)
XLA Ops:
  0.0 2.0 copy.17
  2.0 86.4 %shard_map.82 = (bf16[16,256,1024]{2,1,0:T(8,128)(2,1)}, bf16[16,64,4096]{2,1,0:T(8,128)(2,1)}) custom-call(bf16[256,1024]{1,0:T(8,128)(2,1)} %bitcast.20, bf16[64,4096]{1,0:T(8,128)(2,1)} %bitcast.21), custom_call_target="tpu_custom_call" | custom-call | tf_op jit(solution)/shard_map/pallas_call | solution.py:183
  88.5 1.7 convert_reduce_fusion
  90.2 2.0 fusion.44
  92.1 0.0 copy-start
  92.1 0.0 copy-start.3
  92.2 37.7 %fusion.2.clone.6 = bf16[768,4096]{1,0:T(8,128)(2,1)} fusion(bf16[4096,1024]{1,0:T(8,128)(2,1)} %bitcast.23, f32[4096]{0:T(1024)} %param.14, bf16[768,1024]{1,0:T(8,128)(2,1)} %param.8, f32[1024]{0:T(1024)} %param.12, f32[1024]{0:T(1024)} %param.11, f32[768]{0:T(1024)S(1)} %add_rsqrt_fusion, f32[768]{0:T(1024)S(1)} %broadcast_multiply_fusion), kind=kOutput, calls=%fused_computation.3.clone.clone.clone.clone.clone.1 | convolution fusion | flops 6654787584 | bytes 16283648 | tf_op jit(solution)/shard_map/dot_general | solution.py:211
  129.9 0.0 copy-done
  129.9 0.0 copy-done.3
  129.9 0.0 copy-start.2
  129.9 0.0 copy-start.1
  129.9 9.1 %fusion.48 = bf16[768,1024]{1,0:T(8,128)(2,1)S(1)} fusion(bf16[768,1024]{1,0:T(8,128)(2,1)S(1)} %copy-done, bf16[1024,4096]{1,0:T(8,128)(2,1)S(1)} %bitcast.22, bf16[768,4096]{1,0:T(8,128)(2,1)} %fusion.2.clone.6), kind=kOutput, calls=%fused_computation.60 | convolution fusion | flops 6444810240 | bytes 17825792 | tf_op jit(solution)/shard_map/dot_general | solution.py:214
  139.0 0.0 copy-done.2
  139.0 0.0 copy-done.1
  139.1 0.2 convert_reduce_fusion.1
  139.3 0.7 fusion.59
  140.0 0.9 copy.20.refs_0_
  140.9 41.7 %shard_map.83 = bf16[16,192,1024]{2,1,0:T(8,128)(2,1)} custom-call(bf16[192,1024]{1,0:T(8,128)(2,1)} %copy.20.refs_0_), custom_call_target="tpu_custom_call" | custom-call | tf_op jit(solution)/shard_map/pallas_call | solution.py:183
  182.6 10.7 %convolution_bitcast_fusion.gram_ref = f32[1024,1024]{1,0:T(8,128)S(1)} fusion(bf16[16,192,1024]{2,1,0:T(8,128)(2,1)} %shard_map.83), kind=kOutput, calls=%fused_computation.61 | convolution fusion | flops 6442450944 | bytes 10485760 | tf_op jit(solution)/shard_map/dot_general | solution.py:225
  193.3 0.1 convert_bitcast_fusion.rows_ref
  193.4 63.4 %shard_map.84 = f32[1024,192]{1,0:T(8,128)S(1)} custom-call(f32[1024,1024]{1,0:T(8,128)S(1)} %convolution_bitcast_fusion.gram_ref, f32[1024,192]{1,0:T(8,128)S(1)} %convert_bitcast_fusion.rows_ref), custom_call_target="tpu_custom_call" | custom-call | tf_op jit(solution)/shard_map/pallas_call | solution.py:87
  256.8 1.2 copy.21
  (5 shorter events, 0.1 us)
Async XLA Ops:
  92.1 37.7 %copy-start = (bf16[768,1024]{1,0:T(8,128)(2,1)S(1)}, bf16[768,1024]{1,0:T(8,128)(2,1)}, u32[]{:S(2)}) copy-start(bf16[768,1024]{1,0:T(8,128)(2,1)} %param.8) | copy-start | bytes 4718596
  92.1 37.7 %copy-start.3 = (bf16[16,64,4096]{2,1,0:T(8,128)(2,1)S(1)}, bf16[16,64,4096]{2,1,0:T(8,128)(2,1)}, u32[]{:S(2)}) copy-start(bf16[16,64,4096]{2,1,0:T(8,128)(2,1)} %get-tuple-element.8) | copy-start | bytes 25165828
  129.9 9.1 %copy-start.2 = (s32[1,768]{1,0:T(1,128)S(1)}, s32[1,768]{1,0:T(1,128)}, u32[]{:S(2)}) copy-start(s32[1,768]{1,0:T(1,128)} %param.10) | copy-start | bytes 9220
  129.9 9.1 %copy-start.1 = (s32[1,768]{1,0:T(1,128)S(1)}, s32[1,768]{1,0:T(1,128)}, u32[]{:S(2)}) copy-start(s32[1,768]{1,0:T(1,128)} %param.9) | copy-start | bytes 9220

commit v3 on v2

--- a/solution.py
+++ b/solution.py
@@ -98,9 +98,13 @@
     )(gram, rows_t)
 
 
-def ring_kernel(chips, count, *refs):
-    ins, outs = refs[:count], refs[count : 2 * count]
-    ring_send, ring_recv, core_send, core_recv, own_sem = refs[2 * count :]
+def ring_kernel(chips, count, fused, *refs):
+    if fused:
+        normed, bias, up, down, hidden, down_out, up_out = refs[:7]
+        ins, outs, refs = (up, down), (up_out, down_out), refs[7:]
+    else:
+        ins, outs, refs = refs[:count], refs[count : 2 * count], refs[2 * count :]
+    ring_send, ring_recv, core_send, core_recv, own_sem = refs
     me = lax.axis_index("dp")
     core, chip = lax.rem(me, 2), me // 2
     half = chips // 2
@@ -148,16 +152,59 @@
             device_id_type=pl.DeviceIdType.MESH,
         )
         copy.start()
-        across.append(copy)
+        if fused and a == 0:
+            first[index] = copy
+        else:
+            across.append(copy)
+
+    def compute(slot, block):
+        size = block.shape[0]
+        columns = pl.ds(pl.multiple_of(slot * size, BLOCK), size)
+        tile = normed.shape[0] // 3
+
+        def part(t, carry):
+            at = pl.ds(pl.multiple_of(t * tile, tile), tile)
+            before = lax.dot_general(
+                normed[at, :],
+                block[...],
+                (((1,), (1,)), ((), ())),
+                preferred_element_type=jnp.float32,
+            )
+            before = before + bias[slot]
+            hidden[at, columns] = (
+                0.5 * before * (1.0 + lax.erf(before * math.sqrt(0.5)))
+            ).astype(hidden.dtype)
+            return carry
+
+        lax.fori_loop(0, 3, part, 0)
+
+    first = {}
+
+    def partner_block(index, step, way):
+        first[index].wait_recv()
+        slot = partner
+        if index:
+            slot = device(place + (1 + step) * turn * (1 - 2 * way)) + turn
+        compute(slot, outs[0].at[slot])
 
     flying, local = {}, []
     for a in range(count):
         for way in range(2):
             flying[a, way] = send(a, ins[a], me, way, 0)
         share(a, ins[a], me, 0)
-        local.append(pltpu.make_async_copy(ins[a], outs[a].at[me], own_sem.at[a]))
-        local[-1].start()
+        if not (fused and a == 0):
+            local.append(pltpu.make_async_copy(ins[a], outs[a].at[me], own_sem.at[a]))
+            local[-1].start()
+    if fused:
+        compute(me, ins[0])
     for step in range(half):
+        landed = []
+        if fused:
+            if step == 0:
+                partner_block(0, 0, 0)
+            for way in range(2):
+                if 0 < step <= steps[way]:
+                    partner_block(way * half + step, step - 1, way)
         for a in range(count):
             for way in range(2):
                 if step >= steps[way]:
@@ -168,6 +215,16 @@
                 if step + 1 < steps[way]:
                     flying[a, way] = send(a, block, slot, way, step + 1)
                 share(a, block, slot, 1 + way * half + step)
+                if fused and a == 0:
+                    landed.append((slot, block))
+        for slot, block in landed:
+            compute(slot, block)
+    if fused:
+        for way in range(2):
+            if steps[way] == half:
+                partner_block(way * half + half, half - 1, way)
+        for copy in first.values():
+            copy.wait_send()
     for copy in local:
         copy.wait()
     for copy in started:
@@ -181,7 +238,7 @@
     chips, count = devices // 2, len(blocks)
     dma = pltpu.SemaphoreType.DMA
     return pl.pallas_call(
-        functools.partial(ring_kernel, chips, count),
+        functools.partial(ring_kernel, chips, count, False),
         out_shape=[jax.ShapeDtypeStruct((devices,) + b.shape, b.dtype) for b in blocks],
         in_specs=[pl.BlockSpec(memory_space=pl.ANY)] * count,
         out_specs=[pl.BlockSpec(memory_space=pl.ANY)] * count,
@@ -196,6 +253,34 @@
     )(*blocks)
 
 
+def ring_up(normed, bias, up, down, collective_id):
+    devices = lax.axis_size("dp")
+    chips = devices // 2
+    dma = pltpu.SemaphoreType.DMA
+    whole = pl.BlockSpec(memory_space=pltpu.VMEM)
+    apart = pl.BlockSpec(memory_space=pl.ANY)
+    return pl.pallas_call(
+        functools.partial(ring_kernel, chips, 2, True),
+        out_shape=[
+            jax.ShapeDtypeStruct((normed.shape[0], devices * up.shape[0]), normed.dtype),
+            jax.ShapeDtypeStruct((devices,) + down.shape, down.dtype),
+        ],
+        in_specs=[whole, whole, whole, apart],
+        out_specs=[whole, apart],
+        scratch_shapes=[
+            pltpu.VMEM((devices,) + up.shape, up.dtype),
+            dma((2, 2, chips // 2)),
+            dma((2, 2, chips // 2)),
+            dma((2, chips)),
+            dma((2, chips)),
+            dma((2,)),
+        ],
+        compiler_params=pltpu.CompilerParams(
+            collective_id=collective_id, has_side_effects=True, vmem_limit_bytes=40 << 20
+        ),
+    )(normed, bias.reshape(devices, 1, -1), up, down)
+
+
 def on_device(tokens, token_mask, span_ids, norm_gain, norm_shift, w_up, b_up, w_down):
     values = tokens.astype(jnp.float32)
     center = jnp.mean(values, axis=1, keepdims=True)
@@ -203,14 +288,18 @@
     normed = ((values - center) * lax.rsqrt(spread + 1e-05) * norm_gain + norm_shift).astype(
         jnp.bfloat16
     )
-    up_full, down_full = ring_gather((w_up.T, w_down.T), 0)
     width, hidden_size = tokens.shape[1], b_up.shape[0]
-    up_full, down_full = up_full.reshape(hidden_size, width), down_full.reshape(width, hidden_size)
     over_last = (((1,), (1,)), ((), ()))
-    before = (
-        lax.dot_general(normed, up_full, over_last, preferred_element_type=jnp.float32) + b_up
-    )
-    hidden = jax.nn.gelu(before, approximate=False).astype(jnp.bfloat16)
+    if w_up.shape[1] % BLOCK == 0:
+        hidden, down_full = ring_up(normed, b_up, w_up.T, w_down.T, 0)
+    else:
+        up_full, down_full = ring_gather((w_up.T, w_down.T), 0)
+        up_full = up_full.reshape(hidden_size, width)
+        before = (
+            lax.dot_general(normed, up_full, over_last, preferred_element_type=jnp.float32) + b_up
+        )
+        hidden = jax.nn.gelu(before, approximate=False).astype(jnp.bfloat16)
+    down_full = down_full.reshape(width, hidden_size)
     projected = lax.dot_general(
         hidden, down_full, over_last, preferred_element_type=jnp.float32
     )

time: 258 us -> 225 us (0.87)
  matrix products: 58.2 us -> 23.7 us
    dot_general x2 -> x0, matrix products: 46.8 us -> none  [the longest x1 37.7 us: on_device(): lax.dot_general(normed, up_full, over_last, preferred_element_type=jnp.fl...]
    dot_general x1, matrix products: 0.73 us -> 12.9 us  [on_device(): jnp.dot(select.astype(jnp.bfloat16), block_out, preferred_element_type=jn...]
where the time goes in v3:
time: 225 us; the launch traced here: 224 us
  Pallas kernels  191 us (85%)
  matrix products  23.7 us (11%)
  local copies, waits for them, and re-layouts  5.09 us (2%)
  other arithmetic  4.79 us (2%)
    pallas_call x1, Pallas kernels, ring_up(): pl.pallas_call(functools.partial(ring_kernel, chips, 2, True), out_shape=...  86.5 us
    pallas_call x1, Pallas kernels, whiten(): pl.pallas_call(functools.partial(whiten_kernel, scale), out_shape=jax.Sha...  63.4 us
    pallas_call x1, Pallas kernels, ring_gather(): pl.pallas_call(functools.partial(ring_kernel, chips, count, False), out_s...  40.8 us
    dot_general x1, matrix products, on_device(): jnp.dot(select.astype(jnp.bfloat16), block_out, preferred_element_type=jn...  12.9 us
    dot_general x1, matrix products, on_device(): lax.dot_general(every, every, (((0,), (0,)), ((), ())), preferred_element...  10.9 us

profile of v3, /device:TPU:0, one launch (start us, length us, event | category | flops | bytes accessed | tf_op | source)
XLA Modules:
  0.0 224.5 jit_solution(7246783576177082957)
XLA Ops:
  0.0 1.8 convert_reduce_fusion
  1.8 0.0 copy-start.1
  1.9 2.0 fusion.2
  3.9 0.0 copy-done.3
  3.9 0.0 copy-done.6
  3.9 0.0 copy-done.5
  3.9 0.0 copy-start.8
  3.9 0.0 copy-start.7
  4.0 0.6 fusion.5.refs_0_
  4.6 0.0 copy-done.4
  4.6 0.2 copy.17
  4.8 0.0 copy-done
  4.8 0.0 copy-done.1
  4.8 86.5 %shard_map.82 = (bf16[768,4096]{1,0:T(8,128)(2,1)S(1)}, bf16[16,64,4096]{2,1,0:T(8,128)(2,1)}) custom-call(bf16[768,1024]{1,0:T(8,128)(2,1)S(1)} %fusion.5.refs_0_, f32[16,1,256]{2,1,0:T(1,128)S(1)} %bitcast.16, bf16[256,1024]{1,0:T(8,128)(2,1)S(1)} %bitcast.14, bf16[64,4096]{1,0:T(8,128)(2,1)S(1)} %bitcast.15), custom_call_target="tpu_custom_call" | custom-call | tf_op jit(solution)/shard_map/pallas_call | solution.py:262
  91.4 0.0 copy-start.2
  91.4 2.7 %copy-done.2 = bf16[768,4096]{1,0:T(8,128)(2,1)} copy-done((bf16[768,4096]{1,0:T(8,128)(2,1)}, bf16[768,4096]{1,0:T(8,128)(2,1)S(1)}, u32[]{:S(2)}) %copy-start.2) | copy-done | bytes 6291480
  94.1 0.2 convert_reduce_fusion.1
  94.3 12.9 %fusion.7 = bf16[192,1024]{0,1:T(8,128)(2,1)S(1)} fusion(bf16[768,1024]{1,0:T(8,128)(2,1)} %param.8, bf16[768,4096]{1,0:T(8,128)(2,1)} %copy-done.2, bf16[1024,4096]{1,0:T(8,128)(2,1)} %bitcast.17, f32[192]{0:T(256)S(1)} %broadcast_maximum_fusion, s32[768]{0:T(1024)S(1)} %reduce, pred[768]{0:T(1024)(128)(4,1)S(1)} %compare_reduce_fusion), kind=kOutput, calls=%fused_computation.12 | convolution fusion | flops 6747488256 | bytes 16650752 | tf_op jit(solution)/shard_map/dot_general | solution.py:309
  107.2 0.9 copy.20.refs_0_
  108.1 40.8 %shard_map.83 = bf16[16,192,1024]{2,1,0:T(8,128)(2,1)} custom-call(bf16[192,1024]{1,0:T(8,128)(2,1)} %copy.20.refs_0_), custom_call_target="tpu_custom_call" | custom-call | tf_op jit(solution)/shard_map/pallas_call | solution.py:240
  148.9 10.9 %convolution_bitcast_fusion.gram_ref = f32[1024,1024]{1,0:T(8,128)S(1)} fusion(bf16[16,192,1024]{2,1,0:T(8,128)(2,1)} %shard_map.83), kind=kOutput, calls=%fused_computation.10 | convolution fusion | flops 6442450944 | bytes 10485760 | tf_op jit(solution)/shard_map/dot_general | solution.py:314
  159.8 0.1 convert_bitcast_fusion.rows_ref
  159.9 63.4 %shard_map.84 = f32[1024,192]{1,0:T(8,128)S(1)} custom-call(f32[1024,1024]{1,0:T(8,128)S(1)} %convolution_bitcast_fusion.gram_ref, f32[1024,192]{1,0:T(8,128)S(1)} %convert_bitcast_fusion.rows_ref), custom_call_target="tpu_custom_call" | custom-call | tf_op jit(solution)/shard_map/pallas_call | solution.py:87
  223.3 1.2 copy.21
  (12 shorter events, 0.1 us)
Async XLA Ops:
  0.0 3.9 %copy-start.3 = (bf16[768,1024]{1,0:T(8,128)(2,1)S(1)}, bf16[768,1024]{1,0:T(8,128)(2,1)}, u32[]{:S(2)}) copy-start(bf16[768,1024]{1,0:T(8,128)(2,1)} %param.8) | copy-start | bytes 4718596
  0.0 3.9 %copy-start.6 = (f32[1024]{0:T(1024)S(1)}, f32[1024]{0:T(1024)}, u32[]{:S(2)}) copy-start(f32[1024]{0:T(1024)} %param.11) | copy-start | bytes 12292
  0.0 3.9 %copy-start.5 = (f32[1024]{0:T(1024)S(1)}, f32[1024]{0:T(1024)}, u32[]{:S(2)}) copy-start(f32[1024]{0:T(1024)} %param.12) | copy-start | bytes 12292
  0.0 4.6 %copy-start.4 = (bf16[1024,256]{1,0:T(8,128)(2,1)S(1)}, bf16[1024,256]{1,0:T(8,128)(2,1)}, u32[]{:S(2)}) copy-start(bf16[1024,256]{1,0:T(8,128)(2,1)} %param.13) | copy-start | bytes 1572868
  1.8 3.0 %copy-start = (bf16[4096,64]{0,1:T(8,128)(2,1)S(1)}, bf16[4096,64]{0,1:T(8,128)(2,1)}, u32[]{:S(2)}) copy-start(bf16[4096,64]{0,1:T(8,128)(2,1)} %param.15) | copy-start | bytes 1572868
  1.8 3.0 %copy-start.1 = (f32[4096]{0:T(1024)S(1)}, f32[4096]{0:T(1024)}, u32[]{:S(2)}) copy-start(f32[4096]{0:T(1024)} %param.14) | copy-start | bytes 49156
  3.9 90.2 %copy-start.8 = (s32[1,768]{1,0:T(1,128)S(1)}, s32[1,768]{1,0:T(1,128)}, u32[]{:S(2)}) copy-start(s32[1,768]{1,0:T(1,128)} %param.10) | copy-start | bytes 9220
  3.9 90.2 %copy-start.7 = (s32[1,768]{1,0:T(1,128)S(1)}, s32[1,768]{1,0:T(1,128)}, u32[]{:S(2)}) copy-start(s32[1,768]{1,0:T(1,128)} %param.9) | copy-start | bytes 9220
  91.4 2.7 %copy-start.2 = (bf16[768,4096]{1,0:T(8,128)(2,1)}, bf16[768,4096]{1,0:T(8,128)(2,1)S(1)}, u32[]{:S(2)}) copy-start(bf16[768,4096]{1,0:T(8,128)(2,1)S(1)} %get-tuple-element.7) | copy-start | bytes 18874372

commit v4 on v3

--- a/solution.py
+++ b/solution.py
@@ -68,15 +68,19 @@
         )
         out_ref[pl.ds(lo, BLOCK), :] = panel[:, n : n + extra] * scale
 
-        def trail(i, carry):
-            hi = pl.multiple_of(i * BLOCK, BLOCK)
-            left = panel[:, pl.ds(hi, BLOCK)].T
-            a[pl.ds(hi, BLOCK), :] -= jnp.dot(
-                left, panel[...], preferred_element_type=jnp.float32, precision=HIGHEST
-            )
-            return carry
-
-        return lax.fori_loop(k + 1, blocks, trail, carry)
+        for first in range(0, blocks, 2):
+            start = first * BLOCK
+
+            def trail(i, carry, start=start):
+                hi = pl.multiple_of(i * BLOCK, BLOCK)
+                left = panel[:, pl.ds(hi, BLOCK)].T
+                a[pl.ds(hi, BLOCK), start:] -= jnp.dot(
+                    left, panel[:, start:], preferred_element_type=jnp.float32, precision=HIGHEST
+                )
+                return carry
+
+            lax.fori_loop(jnp.maximum(k + 1, first), min(first + 2, blocks), trail, 0)
+        return carry
 
     lax.fori_loop(0, blocks, step, 0)
 

time: 225 us -> 218 us (0.969)
  Pallas kernels: 191 us -> 184 us
    pallas_call x1, Pallas kernels: 63.4 us -> 57 us  [whiten(): pl.pallas_call(functools.partial(whiten_kernel, scale), out_shape=jax.Sha...]
where the time goes in v4:
time: 218 us
  Pallas kernels  184 us (84%)
  matrix products  23.7 us (11%)
  local copies, waits for them, and re-layouts  5.09 us (2%)
  other arithmetic  4.79 us (2%)
    pallas_call x1, Pallas kernels, ring_up(): pl.pallas_call(functools.partial(ring_kernel, chips, 2, True), out_shape=...  86.5 us
    pallas_call x1, Pallas kernels, whiten(): pl.pallas_call(functools.partial(whiten_kernel, scale), out_shape=jax.Sha...  57 us
    pallas_call x1, Pallas kernels, ring_gather(): pl.pallas_call(functools.partial(ring_kernel, chips, count, False), out_s...  40.8 us
    dot_general x1, matrix products, on_device(): jnp.dot(select.astype(jnp.bfloat16), block_out, preferred_element_type=jn...  12.9 us
    dot_general x1, matrix products, on_device(): lax.dot_general(every, every, (((0,), (0,)), ((), ())), preferred_element...  10.9 us

profile of v4, /device:TPU:0, one launch (start us, length us, event | category | flops | bytes accessed | tf_op | source)
XLA Modules:
  0.0 218.1 jit_solution(7489782415812673230)
XLA Ops:
  0.0 1.8 convert_reduce_fusion
  1.8 0.0 copy-start.1
  1.9 2.0 fusion.2
  3.9 0.0 copy-done.3
  3.9 0.0 copy-done.6
  3.9 0.0 copy-done.5
  3.9 0.0 copy-start.8
  3.9 0.0 copy-start.7
  4.0 0.6 fusion.5.refs_0_
  4.6 0.0 copy-done.4
  4.6 0.2 copy.17
  4.8 0.0 copy-done
  4.8 0.0 copy-done.1
  4.8 86.5 %shard_map.82 = (bf16[768,4096]{1,0:T(8,128)(2,1)S(1)}, bf16[16,64,4096]{2,1,0:T(8,128)(2,1)}) custom-call(bf16[768,1024]{1,0:T(8,128)(2,1)S(1)} %fusion.5.refs_0_, f32[16,1,256]{2,1,0:T(1,128)S(1)} %bitcast.16, bf16[256,1024]{1,0:T(8,128)(2,1)S(1)} %bitcast.14, bf16[64,4096]{1,0:T(8,128)(2,1)S(1)} %bitcast.15), custom_call_target="tpu_custom_call" | custom-call | tf_op jit(solution)/shard_map/pallas_call | solution.py:266
  91.4 0.0 copy-start.2
  91.4 2.7 %copy-done.2 = bf16[768,4096]{1,0:T(8,128)(2,1)} copy-done((bf16[768,4096]{1,0:T(8,128)(2,1)}, bf16[768,4096]{1,0:T(8,128)(2,1)S(1)}, u32[]{:S(2)}) %copy-start.2) | copy-done | bytes 6291480
  94.1 0.2 convert_reduce_fusion.1
  94.3 12.9 %fusion.7 = bf16[192,1024]{0,1:T(8,128)(2,1)S(1)} fusion(bf16[768,1024]{1,0:T(8,128)(2,1)} %param.8, bf16[768,4096]{1,0:T(8,128)(2,1)} %copy-done.2, bf16[1024,4096]{1,0:T(8,128)(2,1)} %bitcast.17, f32[192]{0:T(256)S(1)} %broadcast_maximum_fusion, s32[768]{0:T(1024)S(1)} %reduce, pred[768]{0:T(1024)(128)(4,1)S(1)} %compare_reduce_fusion), kind=kOutput, calls=%fused_computation.12 | convolution fusion | flops 6747488256 | bytes 16650752 | tf_op jit(solution)/shard_map/dot_general | solution.py:313
  107.2 0.9 copy.20.refs_0_
  108.1 40.8 %shard_map.83 = bf16[16,192,1024]{2,1,0:T(8,128)(2,1)} custom-call(bf16[192,1024]{1,0:T(8,128)(2,1)} %copy.20.refs_0_), custom_call_target="tpu_custom_call" | custom-call | tf_op jit(solution)/shard_map/pallas_call | solution.py:244
  148.9 10.9 %convolution_bitcast_fusion.gram_ref = f32[1024,1024]{1,0:T(8,128)S(1)} fusion(bf16[16,192,1024]{2,1,0:T(8,128)(2,1)} %shard_map.83), kind=kOutput, calls=%fused_computation.10 | convolution fusion | flops 6442450944 | bytes 10485760 | tf_op jit(solution)/shard_map/dot_general | solution.py:318
  159.8 0.1 convert_bitcast_fusion.rows_ref
  159.9 57.0 %shard_map.84 = f32[1024,192]{1,0:T(8,128)S(1)} custom-call(f32[1024,1024]{1,0:T(8,128)S(1)} %convolution_bitcast_fusion.gram_ref, f32[1024,192]{1,0:T(8,128)S(1)} %convert_bitcast_fusion.rows_ref), custom_call_target="tpu_custom_call" | custom-call | tf_op jit(solution)/shard_map/pallas_call | solution.py:91
  216.9 1.2 copy.21
  (12 shorter events, 0.1 us)
Async XLA Ops:
  0.0 3.9 %copy-start.3 = (bf16[768,1024]{1,0:T(8,128)(2,1)S(1)}, bf16[768,1024]{1,0:T(8,128)(2,1)}, u32[]{:S(2)}) copy-start(bf16[768,1024]{1,0:T(8,128)(2,1)} %param.8) | copy-start | bytes 4718596
  0.0 3.9 %copy-start.6 = (f32[1024]{0:T(1024)S(1)}, f32[1024]{0:T(1024)}, u32[]{:S(2)}) copy-start(f32[1024]{0:T(1024)} %param.11) | copy-start | bytes 12292
  0.0 3.9 %copy-start.5 = (f32[1024]{0:T(1024)S(1)}, f32[1024]{0:T(1024)}, u32[]{:S(2)}) copy-start(f32[1024]{0:T(1024)} %param.12) | copy-start | bytes 12292
  0.0 4.6 %copy-start.4 = (bf16[1024,256]{1,0:T(8,128)(2,1)S(1)}, bf16[1024,256]{1,0:T(8,128)(2,1)}, u32[]{:S(2)}) copy-start(bf16[1024,256]{1,0:T(8,128)(2,1)} %param.13) | copy-start | bytes 1572868
  1.8 3.0 %copy-start = (bf16[4096,64]{0,1:T(8,128)(2,1)S(1)}, bf16[4096,64]{0,1:T(8,128)(2,1)}, u32[]{:S(2)}) copy-start(bf16[4096,64]{0,1:T(8,128)(2,1)} %param.15) | copy-start | bytes 1572868
  1.8 3.0 %copy-start.1 = (f32[4096]{0:T(1024)S(1)}, f32[4096]{0:T(1024)}, u32[]{:S(2)}) copy-start(f32[4096]{0:T(1024)} %param.14) | copy-start | bytes 49156
  3.9 90.2 %copy-start.8 = (s32[1,768]{1,0:T(1,128)S(1)}, s32[1,768]{1,0:T(1,128)}, u32[]{:S(2)}) copy-start(s32[1,768]{1,0:T(1,128)} %param.10) | copy-start | bytes 9220
  3.9 90.2 %copy-start.7 = (s32[1,768]{1,0:T(1,128)S(1)}, s32[1,768]{1,0:T(1,128)}, u32[]{:S(2)}) copy-start(s32[1,768]{1,0:T(1,128)} %param.9) | copy-start | bytes 9220
  91.4 2.7 %copy-start.2 = (bf16[768,4096]{1,0:T(8,128)(2,1)}, bf16[768,4096]{1,0:T(8,128)(2,1)S(1)}, u32[]{:S(2)}) copy-start(bf16[768,4096]{1,0:T(8,128)(2,1)S(1)} %get-tuple-element.7) | copy-start | bytes 18874372

commit v5 on v4

--- a/solution.py
+++ b/solution.py
@@ -51,10 +51,14 @@
             held[q] = total
 
 
-def whiten_kernel(scale, gram_ref, rows_ref, out_ref, a, panel, inv):
-    n = gram_ref.shape[0]
+def whiten_kernel(scale, first_ref, cross_ref, last_ref, rows_ref, out_ref, a, panel, inv):
+    half = first_ref.shape[0]
+    n = 2 * half
     extra = rows_ref.shape[1]
-    a[:, :n] = gram_ref[...]
+    a[:half, :half] = first_ref[...]
+    a[:half, half:n] = cross_ref[...]
+    a[half:, :half] = jnp.zeros((half, half), jnp.float32)
+    a[half:, half:n] = last_ref[...]
     a[:, n:] = jnp.zeros((n, a.shape[1] - n), jnp.float32)
     a[:, n : n + extra] = rows_ref[...]
     blocks = n // BLOCK
@@ -91,7 +95,7 @@
     return pl.pallas_call(
         functools.partial(whiten_kernel, scale),
         out_shape=jax.ShapeDtypeStruct((n, extra), jnp.float32),
-        in_specs=[pl.BlockSpec(memory_space=pltpu.VMEM)] * 2,
+        in_specs=[pl.BlockSpec(memory_space=pltpu.VMEM)] * 4,
         out_specs=pl.BlockSpec(memory_space=pltpu.VMEM),
         scratch_shapes=[
             pltpu.VMEM((n, wide), jnp.float32),
@@ -99,7 +103,7 @@
             pltpu.VMEM((BLOCK, BLOCK), jnp.float32),
         ],
         compiler_params=pltpu.CompilerParams(vmem_limit_bytes=32 << 20),
-    )(gram, rows_t)
+    )(*gram, rows_t)
 
 
 def ring_kernel(chips, count, fused, *refs):
@@ -313,11 +317,15 @@
     sums = jnp.dot(select.astype(jnp.bfloat16), block_out, preferred_element_type=jnp.float32)
     counts = jnp.sum(select.astype(jnp.float32), axis=1)
     pooled = (sums / jnp.maximum(counts, 1.0)[:, None]).astype(jnp.bfloat16)
-    (every,) = ring_gather((pooled,), 1)
-    every = every.reshape(-1, width)
-    gram = lax.dot_general(
-        every, every, (((0,), (0,)), ((), ())), preferred_element_type=jnp.float32
-    )
+    middle = width // 2
+    left, right = (
+        half.reshape(-1, middle)
+        for half in ring_gather((pooled[:, :middle], pooled[:, middle:]), 1)
+    )
+    gram = [
+        lax.dot_general(one, two, (((0,), (0,)), ((), ())), preferred_element_type=jnp.float32)
+        for one, two in ((left, left), (left, right), (right, right))
+    ]
     total_rows = SEG_DEV * lax.axis_size("dp")
     return whiten(gram, pooled.astype(jnp.float32).T, math.sqrt(total_rows)).T
 

time: 218 us -> 212 us (0.972)
  Pallas kernels: 184 us -> 180 us
  matrix products: 23.7 us -> 21.3 us
    pallas_call x1, Pallas kernels: 40.8 us -> 36.2 us  [ring_gather(): pl.pallas_call(functools.partial(ring_kernel, chips, count, False), out_s...]
    dot_general x1 -> x3, matrix products: 10.9 us -> 8.42 us  [on_device(): lax.dot_general(one, two, (((0,), (0,)), ((), ())), preferred_element_typ...]
where the time goes in v5:
time: 212 us
  Pallas kernels  180 us (85%)
  matrix products  21.3 us (10%)
  local copies, waits for them, and re-layouts  5.85 us (3%)
  other arithmetic  4.79 us (2%)
    pallas_call x1, Pallas kernels, ring_up(): pl.pallas_call(functools.partial(ring_kernel, chips, 2, True), out_shape=...  86.7 us
    pallas_call x1, Pallas kernels, whiten(): pl.pallas_call(functools.partial(whiten_kernel, scale), out_shape=jax.Sha...  57.3 us
    pallas_call x1, Pallas kernels, ring_gather(): pl.pallas_call(functools.partial(ring_kernel, chips, count, False), out_s...  36.2 us
    dot_general x1, matrix products, on_device(): jnp.dot(select.astype(jnp.bfloat16), block_out, preferred_element_type=jn...  12.9 us
    dot_general x3, matrix products, on_device(): lax.dot_general(one, two, (((0,), (0,)), ((), ())), preferred_element_typ...  8.42 us

profile of v5, /device:TPU:0, one launch (start us, length us, event | category | flops | bytes accessed | tf_op | source)
XLA Modules:
  0.0 212.3 jit_solution(4466447594820052112)
XLA Ops:
  0.0 1.8 convert_reduce_fusion
  1.8 0.0 copy-start.1
  1.9 2.0 fusion.2
  3.9 0.0 copy-done.5
  3.9 0.0 copy-start.10
  3.9 0.0 copy-start.9
  4.0 0.6 fusion.5.refs_0_
  4.6 0.0 copy-done.6
  4.6 0.2 copy.14
  4.8 86.7 %shard_map.82 = (bf16[768,4096]{1,0:T(8,128)(2,1)S(1)}, bf16[16,64,4096]{2,1,0:T(8,128)(2,1)}) custom-call(bf16[768,1024]{1,0:T(8,128)(2,1)S(1)} %fusion.5.refs_0_, f32[16,1,256]{2,1,0:T(1,128)S(1)} %bitcast.24, bf16[256,1024]{1,0:T(8,128)(2,1)S(1)} %bitcast.22, bf16[64,4096]{1,0:T(8,128)(2,1)S(1)} %bitcast.23), custom_call_target="tpu_custom_call" | custom-call | tf_op jit(solution)/shard_map/pallas_call | solution.py:270
  91.6 2.7 %copy-done.2 = bf16[768,4096]{1,0:T(8,128)(2,1)} copy-done((bf16[768,4096]{1,0:T(8,128)(2,1)}, bf16[768,4096]{1,0:T(8,128)(2,1)S(1)}, u32[]{:S(2)}) %copy-start.2) | copy-done | bytes 6291480
  94.3 0.0 copy-done.10
  94.3 0.2 convert_reduce_fusion.1
  94.5 12.9 %fusion.7 = bf16[192,1024]{0,1:T(8,128)(2,1)S(1)} fusion(bf16[768,1024]{1,0:T(8,128)(2,1)} %param.8, bf16[768,4096]{1,0:T(8,128)(2,1)} %copy-done.2, bf16[1024,4096]{1,0:T(8,128)(2,1)} %bitcast.25, f32[192]{0:T(256)S(1)} %broadcast_maximum_fusion, s32[768]{0:T(1024)S(1)} %reduce, pred[768]{0:T(1024)(128)(4,1)S(1)} %compare_reduce_fusion), kind=kOutput, calls=%fused_computation.14 | convolution fusion | flops 6747488256 | bytes 16650752 | tf_op jit(solution)/shard_map/dot_general | solution.py:317
  107.4 0.8 copy.16.refs_0_
  108.2 0.8 copy.17.refs_1_
  109.0 36.2 %shard_map.83 = (bf16[16,192,512]{2,1,0:T(8,128)(2,1)}, bf16[16,192,512]{2,1,0:T(8,128)(2,1)}) custom-call(bf16[192,512]{1,0:T(8,128)(2,1)} %copy.16.refs_0_, bf16[192,512]{1,0:T(8,128)(2,1)} %copy.17.refs_1_), custom_call_target="tpu_custom_call" | custom-call | tf_op jit(solution)/shard_map/pallas_call | solution.py:248
  145.2 4.8 %convolution_bitcast_fusion.1.cross_ref = f32[512,512]{1,0:T(8,128)S(1)} fusion(bf16[16,192,512]{2,1,0:T(8,128)(2,1)} %get-tuple-element.11, bf16[16,192,512]{2,1,0:T(8,128)(2,1)} %get-tuple-element.12), kind=kOutput, calls=%fused_computation.11 | convolution fusion | flops 1610612736 | bytes 7340032 | tf_op jit(solution)/shard_map/dot_general | solution.py:326
  150.1 1.8 convolution_bitcast_fusion.last_ref
  151.9 0.1 copy-done.3
  151.9 1.8 convolution_bitcast_fusion.2.first_ref
  153.8 0.1 convert_bitcast_fusion.rows_ref
  153.8 57.3 %shard_map.84 = f32[1024,192]{1,0:T(8,128)S(1)} custom-call(f32[512,512]{1,0:T(8,128)S(1)} %convolution_bitcast_fusion.2.first_ref, f32[512,512]{1,0:T(8,128)S(1)} %convolution_bitcast_fusion.1.cross_ref, f32[512,512]{1,0:T(8,128)S(1)} %convolution_bitcast_fusion.last_ref, f32[1024,192]{1,0:T(8,128)S(1)} %convert_bitcast_fusion.rows_ref), custom_call_target="tpu_custom_call" | custom-call | tf_op jit(solution)/shard_map/pallas_call | solution.py:95
  211.1 1.2 copy.18
  (20 shorter events, 0.1 us)
Async XLA Ops:
  0.0 3.9 %copy-start.5 = (bf16[768,1024]{1,0:T(8,128)(2,1)S(1)}, bf16[768,1024]{1,0:T(8,128)(2,1)}, u32[]{:S(2)}) copy-start(bf16[768,1024]{1,0:T(8,128)(2,1)} %param.8) | copy-start | bytes 4718596
  0.0 3.9 %copy-start.8 = (f32[1024]{0:T(1024)S(1)}, f32[1024]{0:T(1024)}, u32[]{:S(2)}) copy-start(f32[1024]{0:T(1024)} %param.11) | copy-start | bytes 12292
  0.0 3.9 %copy-start.7 = (f32[1024]{0:T(1024)S(1)}, f32[1024]{0:T(1024)}, u32[]{:S(2)}) copy-start(f32[1024]{0:T(1024)} %param.12) | copy-start | bytes 12292
  0.0 4.6 %copy-start.6 = (bf16[1024,256]{1,0:T(8,128)(2,1)S(1)}, bf16[1024,256]{1,0:T(8,128)(2,1)}, u32[]{:S(2)}) copy-start(bf16[1024,256]{1,0:T(8,128)(2,1)} %param.13) | copy-start | bytes 1572868
  1.8 3.0 %copy-start = (bf16[4096,64]{0,1:T(8,128)(2,1)S(1)}, bf16[4096,64]{0,1:T(8,128)(2,1)}, u32[]{:S(2)}) copy-start(bf16[4096,64]{0,1:T(8,128)(2,1)} %param.15) | copy-start | bytes 1572868
  1.8 3.0 %copy-start.1 = (f32[4096]{0:T(1024)S(1)}, f32[4096]{0:T(1024)}, u32[]{:S(2)}) copy-start(f32[4096]{0:T(1024)} %param.14) | copy-start | bytes 49156
  3.9 90.4 %copy-start.10 = (s32[1,768]{1,0:T(1,128)S(1)}, s32[1,768]{1,0:T(1,128)}, u32[]{:S(2)}) copy-start(s32[1,768]{1,0:T(1,128)} %param.10) | copy-start | bytes 9220
  3.9 90.4 %copy-start.9 = (s32[1,768]{1,0:T(1,128)S(1)}, s32[1,768]{1,0:T(1,128)}, u32[]{:S(2)}) copy-start(s32[1,768]{1,0:T(1,128)} %param.9) | copy-start | bytes 9220
  91.6 2.7 %copy-start.2 = (bf16[768,4096]{1,0:T(8,128)(2,1)}, bf16[768,4096]{1,0:T(8,128)(2,1)S(1)}, u32[]{:S(2)}) copy-start(bf16[768,4096]{1,0:T(8,128)(2,1)S(1)} %get-tuple-element.9) | copy-start | bytes 18874372
  145.2 4.8 %copy-start.4 = (bf16[16,192,512]{2,1,0:T(8,128)(2,1)S(1)}, bf16[16,192,512]{2,1,0:T(8,128)(2,1)}, u32[]{:S(2)}) copy-start(bf16[16,192,512]{2,1,0:T(8,128)(2,1)} %get-tuple-element.12) | copy-start | bytes 9437188
  150.0 1.9 copy-start.3
